TPU v7x, 32 devices: a whole 2x2x4 slice. The times are simulated.
32 devices in a mesh: row: 4 (over x, core), col: 8 (over z, y).
Axes of the slice: x: 2, y: 2, z: 4, core: 2. Of those that a mesh axis runs over, the one named last changes fastest.
Arguments:
- tile_list: int32 [512, 2], P(('row', 'col')), may hold values from -1 to 63, as said below
- tile_values: bfloat16 [512, 512, 512], P(('row', 'col'))
- block_order: int32 [64], replicated, may hold values from 0 to 63, as said below
- basis: bfloat16 [64, 512, 256], P(('row', 'col')), may hold values from -8 to 8
Outputs:
- basis_out: bfloat16 [64, 512, 256], P(('row', 'col'))
- projected: float32 [256, 256], replicated
Inputs may be any that keep to these rules, and one draw needn't show every extreme that they name: `block_order`: A permutation of the channel blocks; slot p lies on device p // 2 in row-major order of (row, col). `tile_list`: slots of device (i, j) hold tiles whose row block sits in a slot of a device of row index i and whose column block sits in a slot of a device of column index j; each unordered pair of blocks appears at most once in all; empty slots hold -1 in both columns and may stand anywhere among a device's slots; every device holds at most 16 tiles and some device holds exactly 16.
All inputs are finite; a program needn't handle non-finite values.
Results may differ from a plain program's by a relative error of at most 0.0017.
Values may be sent and summed in bfloat16 or wider, within the bound.
A program may use at most 128 MiB of HBM per device.

v0:
```python
import jax
import jax.numpy as jnp
from jax import lax
from jax.sharding import PartitionSpec as P


def per_device(tile_list, tile_values, block_order, basis):
    rows_count = lax.axis_size("row")
    cols_count = lax.axis_size("col")
    own_blocks = basis.shape[0]
    edge = basis.shape[1]
    rank = basis.shape[2]
    blocks_all = block_order.shape[0]
    scale = jnp.sqrt(jnp.float32(blocks_all * edge))
    row_here = lax.axis_index("row")
    row_group = own_blocks * cols_count
    col_group = own_blocks * rows_count
    present = tile_list[:, 0] >= 0
    slot_range = jnp.arange(blocks_all, dtype=jnp.int32)
    ids_both = jnp.where(present[:, None], tile_list, 0)
    match = block_order[None, None, :] == ids_both[:, :, None]
    slots_both = jnp.sum(jnp.where(match, slot_range[None, None, :], 0), axis=2)
    first_slot = slots_both[:, 0]
    second_slot = slots_both[:, 1]
    row_local = jnp.where(present, first_slot - row_here * row_group, row_group)
    owner_second = second_slot // own_blocks
    col_local = jnp.where(
        present, owner_second // cols_count * own_blocks + second_slot % own_blocks, col_group
    )
    column_side = lax.all_gather(basis, "row", axis=0, tiled=True)
    row_side = lax.all_gather(basis, "col", axis=0, tiled=True)
    empty_block = jnp.zeros((1, edge, rank), basis.dtype)
    column_padded = jnp.concatenate([column_side, empty_block], axis=0)
    row_padded = jnp.concatenate([row_side, empty_block], axis=0)
    picked_col = column_padded[col_local]
    picked_row = row_padded[row_local]
    near_prod = jnp.einsum(
        "tab,tbk->tak", tile_values, picked_col, preferred_element_type=jnp.float32
    )
    far_prod = jnp.einsum(
        "tba,tbk->tak", tile_values, picked_row, preferred_element_type=jnp.float32
    )
    col_partial = (
        jnp.zeros((col_group, edge, rank), jnp.float32).at[col_local].add(far_prod, mode="drop")
    )
    row_partial = (
        jnp.zeros((row_group, edge, rank), jnp.float32).at[row_local].add(near_prod, mode="drop")
    )
    row_owned = lax.psum_scatter(row_partial, "col", scatter_dimension=0, tiled=True)
    upper_part = lax.optimization_barrier(col_partial.astype(jnp.bfloat16))
    remainder = col_partial - upper_part.astype(jnp.float32)
    middle_part = lax.optimization_barrier(remainder.astype(jnp.bfloat16))
    lower_part = (remainder - middle_part.astype(jnp.float32)).astype(jnp.bfloat16)
    pieces = jnp.concatenate([upper_part, middle_part, lower_part], axis=2)
    folded = jnp.einsum("sak,saj->kj", column_side, pieces, preferred_element_type=jnp.float32)
    tile_form = folded[:, :rank] + folded[:, rank : 2 * rank] + folded[:, 2 * rank :]
    projected = lax.psum((tile_form + tile_form.T) / scale, ("row", "col"))
    col_owned = lax.psum_scatter(col_partial, "row", scatter_dimension=0, tiled=True)
    product = (row_owned + col_owned).reshape(own_blocks * edge, rank)
    gram_term = jnp.dot(product.T, product, precision=lax.Precision.HIGHEST)
    gram = lax.psum(gram_term, ("row", "col"))
    first_factor = jnp.linalg.cholesky(gram)
    first_basis = lax.linalg.triangular_solve(
        first_factor, product, left_side=False, lower=True, transpose_a=True
    )
    second_term = jnp.dot(first_basis.T, first_basis, precision=lax.Precision.HIGHEST)
    second = lax.psum(second_term, ("row", "col"))
    second_factor = jnp.linalg.cholesky(second)
    final = lax.linalg.triangular_solve(
        second_factor, first_basis, left_side=False, lower=True, transpose_a=True
    )
    basis_out = (final * scale).astype(jnp.bfloat16).reshape(own_blocks, edge, rank)
    return (basis_out, projected)


def solution(mesh):
    in_specs = (
        P(("row", "col"), None),
        P(("row", "col"), None, None),
        P(),
        P(("row", "col"), None, None),
    )
    out_specs = (P(("row", "col"), None, None), P())
    return jax.shard_map(
        per_device, mesh=mesh, in_specs=in_specs, out_specs=out_specs, check_vma=False
    )
```

profile of v0, /device:TPU:0, one launch (start us, length us, event | category | flops | bytes accessed | tf_op | source)
XLA Modules:
  0.0 729.1 jit_solution(8188007919640402378)
XLA Ops:
  11.6 74.0 %all-gather.5.cloned.1.call-done = bf16[16,512,256]{2,1,0:T(8,128)(2,1)} async-done(((bf16[2,512,256]{2,1,0:T(8,128)(2,1)}), bf16[16,512,256]{2,1,0:T(8,128)(2,1)}) %all-gather.5.cloned.1.call-update) | async-done | bytes 4194320 | tf_op jit(solution)/shard_map/all_gather | solution.py:31
  85.6 4.6 concatenate.13
  90.3 5.2 gather_fusion.1
  95.5 10.3 %convolution_bitcast_fusion = f32[16,512,256]{1,2,0:T(8,128)} fusion(bf16[16,512,256]{2,1,0:T(8,128)(2,1)} %gather_fusion.1, bf16[16,512,512]{2,1,0:T(8,128)(2,1)} %param.8), kind=kOutput, calls=%fused_computation.16 | convolution fusion | flops 2147483648 | bytes 20971520 | tf_op jit(solution)/shard_map/tba,tbk->tak/dot_general | solution.py:40
  105.8 9.3 %copy.39 = f32[16,512,256]{2,1,0:T(8,128)} copy(f32[16,512,256]{1,2,0:T(8,128)} %convolution_bitcast_fusion) | data formatting | bytes 16777216 | tf_op jit(solution)/shard_map/tba,tbk->tak/dot_general | solution.py:40
  115.1 2.3 broadcast_in_dim.54
  117.4 15.6 %scatter_fusion.1 = f32[8,512,256]{2,1,0:T(8,128)} fusion(f32[8,512,256]{2,1,0:T(8,128)} %broadcast_in_dim.54, s32[16]{0:T(128)S(1)} %get-tuple-element.46, f32[16,512,256]{2,1,0:T(8,128)} %copy.39), kind=kCustom, calls=%fused_computation.3 | custom fusion | flops 2097152 | bytes 25165888 | tf_op jit(solution)/shard_map/scatter-add | solution.py:44
  133.1 1.7 concatenate.12
  134.9 2.7 gather_fusion
  137.6 12.1 %convolution_bitcast_fusion.1 = f32[16,512,256]{1,2,0:T(8,128)} fusion(bf16[16,512,256]{2,1,0:T(8,128)(2,1)} %gather_fusion, bf16[16,512,512]{2,1,0:T(8,128)(2,1)} %param.8), kind=kOutput, calls=%fused_computation.17 | convolution fusion | flops 2147483648 | bytes 20971520 | tf_op jit(solution)/shard_map/tab,tbk->tak/dot_general | solution.py:37
  149.7 9.3 %copy.37 = f32[16,512,256]{2,1,0:T(8,128)} copy(f32[16,512,256]{1,2,0:T(8,128)} %convolution_bitcast_fusion.1) | data formatting | bytes 16777216 | tf_op jit(solution)/shard_map/tab,tbk->tak/dot_general | solution.py:37
  159.1 4.1 broadcast_in_dim.47
  163.1 15.9 %scatter_fusion = f32[16,512,256]{2,1,0:T(8,128)} fusion(f32[16,512,256]{2,1,0:T(8,128)} %broadcast_in_dim.47, s32[16]{0:T(128)S(1)} %fusion.37, f32[16,512,256]{2,1,0:T(8,128)} %copy.37), kind=kCustom, calls=%fused_computation.2 | custom fusion | flops 2097152 | bytes 25165888 | tf_op jit(solution)/shard_map/scatter-add | solution.py:47
  179.0 12.8 %all-reduce.7.cloned.1.call-start = ((), (), s32[]{:S(2)}) async-start(), calls=%async_computation.6 | async-start | bytes 524288 | tf_op jit(solution)/shard_map/psum | solution.py:61
  191.9 5.4 copy.46
  197.2 2.6 convert_element_type.19
  203.1 1.8 fusion.7
  205.1 124.2 %reduce-scatter.3.cloned.1.call-done = f32[2,512,256]{2,1,0:T(8,128)} async-done(((f32[16,512,256]{2,1,0:T(8,128)}), f32[2,512,256]{2,1,0:T(8,128)}) %reduce-scatter.3.cloned.1.call-update) | async-done | bytes 1048592 | tf_op jit(solution)/shard_map/reduce_scatter | solution.py:49
  331.0 2.5 convolution_bitcast_fusion.2
  334.3 126.6 %all-reduce.7.cloned.1.call-done = f32[256,256]{0,1:T(8,128)} async-done(((f32[256,256]{0,1:T(8,128)}), f32[256,256]{0,1:T(8,128)}) %all-reduce.7.cloned.1.call-update) | async-done | bytes 262160 | tf_op jit(solution)/shard_map/psum | solution.py:61
  463.1 11.7 %cholesky.130 = f32[128,128]{1,0:T(8,128)S(1)} custom-call(f32[128,128]{1,0:T(8,128)S(1)} %cholesky.194), custom_call_target="Cholesky" | custom-call | tf_op jit(solution)/shard_map/jit(cholesky)/cholesky | solution.py:62
  474.9 9.8 %custom-call.13 = f32[1,128,128]{1,2,0:T(8,128)S(1)} custom-call(f32[1,128,128]{2,1,0:T(8,128)S(1)} %get-tuple-element.59), custom_call_target="InvertDiagBlocksLowerTriangular" | custom-call | tf_op jit(solution)/shard_map/jit(cholesky)/cholesky | solution.py:62
  485.1 11.7 %cholesky.147 = f32[128,128]{1,0:T(8,128)S(1)} custom-call(f32[128,128]{1,0:T(8,128)S(1)} %convolution_subtract_fusion.3), custom_call_target="Cholesky" | custom-call | tf_op jit(solution)/shard_map/jit(cholesky)/cholesky | solution.py:62
  499.1 4.1 while.4
  503.2 20.0 %custom-call.14 = f32[2,128,128]{1,2,0:T(8,128)S(1)} custom-call(f32[2,128,128]{2,1,0:T(8,128)S(1)} %get-tuple-element.18), custom_call_target="InvertDiagBlocksLowerTriangular" | custom-call | tf_op jit(solution)/shard_map/triangular_solve/custom-call.0 | solution.py:63
  525.5 1.7 fusion.10
  527.2 128.6 %all-reduce.9.cloned.1.call-done = (f32[256,256]{0,1:T(8,128)}, f32[256,256]{0,1:T(8,128)}) async-done(((f32[256,256]{0,1:T(8,128)}, f32[256,256]{0,1:T(8,128)}), (f32[256,256]{0,1:T(8,128)}, f32[256,256]{0,1:T(8,128)})) %all-reduce.9.cloned.1.call-update) | async-done | bytes 524304 | tf_op jit(solution)/shard_map/psum | solution.py:67
  657.9 11.7 %cholesky.164 = f32[128,128]{1,0:T(8,128)S(1)} custom-call(f32[128,128]{1,0:T(8,128)S(1)} %cholesky.197), custom_call_target="Cholesky" | custom-call | tf_op jit(solution)/shard_map/jit(cholesky)/cholesky | solution.py:68
  669.6 9.8 %custom-call.15 = f32[1,128,128]{1,2,0:T(8,128)S(1)} custom-call(f32[1,128,128]{2,1,0:T(8,128)S(1)} %get-tuple-element.55), custom_call_target="InvertDiagBlocksLowerTriangular" | custom-call | tf_op jit(solution)/shard_map/jit(cholesky)/cholesky | solution.py:68
  679.9 11.9 %cholesky.181 = f32[128,128]{1,0:T(8,128)S(1)} custom-call(f32[128,128]{1,0:T(8,128)S(1)} %convolution_subtract_fusion.2), custom_call_target="Cholesky" | custom-call | tf_op jit(solution)/shard_map/jit(cholesky)/cholesky | solution.py:68
  694.5 4.0 while.5
  698.5 19.7 %custom-call.16 = f32[2,128,128]{1,2,0:T(8,128)S(1)} custom-call(f32[2,128,128]{2,1,0:T(8,128)S(1)} %get-tuple-element.19), custom_call_target="InvertDiagBlocksLowerTriangular" | custom-call | tf_op jit(solution)/shard_map/triangular_solve/custom-call.0 | solution.py:69
  (79 shorter events, 31.9 us)
Async XLA Ops:
  7.2 78.5 %all-gather.5.cloned.1.call-start = ((), (), s32[]{:S(2)}) async-start(), calls=%async_computation.4 | async-start | bytes 4718592 | tf_op jit(solution)/shard_map/all_gather | solution.py:31
  7.9 125.2 %all-gather.3.cloned.1.call-start = ((), (), s32[]{:S(2)}) async-start(), calls=%async_computation.2 | async-start | bytes 2621440 | tf_op jit(solution)/shard_map/all_gather | solution.py:30
  8.6 196.5 %reduce-scatter.5.cloned.1.call-start = ((), (), s32[]{:S(2)}) async-start(), calls=%async_computation.5 | async-start | bytes 5242880 | tf_op jit(solution)/shard_map/reduce_scatter | solution.py:58
  133.0 196.3 %reduce-scatter.3.cloned.1.call-start = ((), (), s32[]{:S(2)}) async-start(), calls=%async_computation.3 | async-start | bytes 9437184 | tf_op jit(solution)/shard_map/reduce_scatter | solution.py:49
  179.0 282.0 %all-reduce.7.cloned.1.call-start = ((), (), s32[]{:S(2)}) async-start(), calls=%async_computation.6 | async-start | bytes 524288 | tf_op jit(solution)/shard_map/psum | solution.py:61
  197.2 3.5 copy-start
  201.5 1.6 copy-start.1
  333.5 322.3 %all-reduce.9.cloned.1.call-start = ((), (), s32[]{:S(2)}) async-start(), calls=%async_computation.7 | async-start | bytes 1048576 | tf_op jit(solution)/shard_map/psum | solution.py:67
  679.7 41.5 %copy-start.2 = (f32[256,256]{0,1:T(8,128)S(1)}, f32[256,256]{0,1:T(8,128)}, u32[]{:S(2)}) copy-start(f32[256,256]{0,1:T(8,128)} %get-tuple-element.43) | copy-start | bytes 786436
Sparse Core Ops, SparseCore 0:
  10.1 75.5 all-gather.4
  87.2 21.0 all-gather.2
  133.1 45.1 reduce-scatter.4
  181.8 147.4 reduce-scatter.2
  335.2 125.7 all-reduce.6
  527.3 128.3 all-reduce.8
where the time goes:
time: 737 us; the launch traced here: 729 us
  waiting for transfers between devices  455 us (62%)
  other arithmetic  152 us (21%)
  local copies, waits for them, and re-layouts  58.5 us (8%)
  matrix products  33.5 us (5%)
  between operations  17.3 us (2%)
  starting transfers between devices  13 us (2%)
    psum x1, waiting for transfers between devices, per_device(): second = lax.psum(second_term, ('row', 'col'))  129 us
    psum x1, waiting for transfers between devices, per_device(): gram = lax.psum(gram_term, ('row', 'col'))  127 us
    reduce_scatter x1, waiting for transfers between devices, per_device(): lax.psum_scatter(row_partial, 'col', scatter_dimension=0, tiled=True)  124 us
    all_gather x1, waiting for transfers between devices, per_device(): row_side = lax.all_gather(basis, 'col', axis=0, tiled=True)  74 us
    another operation x7, other arithmetic, per_device(): second_factor = jnp.linalg.cholesky(second)  34.8 us
    another operation x6, other arithmetic, per_device(): first_factor = jnp.linalg.cholesky(gram)  34 us
    another operation x3, other arithmetic, per_device(): lax.linalg.triangular_solve(first_factor, product, left_side=False, lower...  20 us
    another operation x2, other arithmetic, per_device(): lax.linalg.triangular_solve(second_factor, first_basis, left_side=False,...  19.7 us
  transfers between devices with their start and end apart: 6, of which 4 were waited for; matrix products, arithmetic and copies ran while one was open for 15% of the time, Pallas kernels for 0%

commit v1 on v0

--- a/solution.py
+++ b/solution.py
@@ -64,7 +64,7 @@
         first_factor, product, left_side=False, lower=True, transpose_a=True
     )
     second_term = jnp.dot(first_basis.T, first_basis, precision=lax.Precision.HIGHEST)
-    second = lax.psum(second_term, ("row", "col"))
+    second = jnp.sum(lax.all_gather(second_term, ("row", "col")), axis=0)
     second_factor = jnp.linalg.cholesky(second)
     final = lax.linalg.triangular_solve(
         second_factor, first_basis, left_side=False, lower=True, transpose_a=True

time: 737 us -> 688 us (0.934)
  waiting for transfers between devices: 455 us -> 417 us
  starting transfers between devices: 13 us -> 0.42 us
    psum x1 -> x0, waiting for transfers between devices: 129 us -> none  [per_device(): second = lax.psum(second_term, ('row', 'col'))]
    all_gather x0 -> x1, waiting for transfers between devices: none -> 75.4 us  [per_device(): second = jnp.sum(lax.all_gather(second_term, ('row', 'col')), axis=0)]
    psum x1, starting transfers between devices: 12.8 us -> 0.22 us  [per_device(): gram = lax.psum(gram_term, ('row', 'col'))]
    reduce_scatter x1, waiting for transfers between devices: 124 us -> 136 us  [per_device(): lax.psum_scatter(row_partial, 'col', scatter_dimension=0, tiled=True)]
  transfers between devices with their start and end apart: 6 -> 6, of which waited for: 4 -> 4; matrix products, arithmetic and copies ran while one was open for 15% -> 16% of each run, Pallas kernels for 0% -> 0%
where the time goes in v1:
time: 688 us; the launch traced here: 681 us
  waiting for transfers between devices  417 us (61%)
  other arithmetic  155 us (23%)
  local copies, waits for them, and re-layouts  57.6 us (8%)
  matrix products  33.5 us (5%)
  between operations  17.3 us (3%)
    reduce_scatter x1, waiting for transfers between devices, per_device(): lax.psum_scatter(row_partial, 'col', scatter_dimension=0, tiled=True)  136 us
    psum x1, waiting for transfers between devices, per_device(): gram = lax.psum(gram_term, ('row', 'col'))  130 us
    all_gather x1, waiting for transfers between devices, per_device(): second = jnp.sum(lax.all_gather(second_term, ('row', 'col')), axis=0)  75.4 us
    all_gather x1, waiting for transfers between devices, per_device(): row_side = lax.all_gather(basis, 'col', axis=0, tiled=True)  74 us
    another operation x7, other arithmetic, per_device(): second_factor = jnp.linalg.cholesky(second)  34.8 us
    another operation x6, other arithmetic, per_device(): first_factor = jnp.linalg.cholesky(gram)  33.9 us
    another operation x3, other arithmetic, per_device(): lax.linalg.triangular_solve(first_factor, product, left_side=False, lower...  20.1 us
    another operation x2, other arithmetic, per_device(): lax.linalg.triangular_solve(second_factor, first_basis, left_side=False,...  19.7 us
  transfers between devices with their start and end apart: 6, of which 4 were waited for; matrix products, arithmetic and copies ran while one was open for 16% of the time, Pallas kernels for 0%

profile of v1, /device:TPU:0, one launch (start us, length us, event | category | flops | bytes accessed | tf_op | source)
XLA Modules:
  0.0 680.7 jit_solution(2196165574084479257)
XLA Ops:
  11.6 74.0 %all-gather.7.cloned.1.call-done = bf16[16,512,256]{2,1,0:T(8,128)(2,1)} async-done(((bf16[2,512,256]{2,1,0:T(8,128)(2,1)}), bf16[16,512,256]{2,1,0:T(8,128)(2,1)}) %all-gather.7.cloned.1.call-update) | async-done | bytes 4194320 | tf_op jit(solution)/shard_map/all_gather | solution.py:31
  85.6 4.6 concatenate.13
  90.3 5.2 gather_fusion.1
  95.5 10.3 %convolution_bitcast_fusion = f32[16,512,256]{1,2,0:T(8,128)} fusion(bf16[16,512,256]{2,1,0:T(8,128)(2,1)} %gather_fusion.1, bf16[16,512,512]{2,1,0:T(8,128)(2,1)} %param.8), kind=kOutput, calls=%fused_computation.16 | convolution fusion | flops 2147483648 | bytes 20971520 | tf_op jit(solution)/shard_map/tba,tbk->tak/dot_general | solution.py:40
  105.8 9.3 %copy.37 = f32[16,512,256]{2,1,0:T(8,128)} copy(f32[16,512,256]{1,2,0:T(8,128)} %convolution_bitcast_fusion) | data formatting | bytes 16777216 | tf_op jit(solution)/shard_map/tba,tbk->tak/dot_general | solution.py:40
  115.1 2.3 broadcast_in_dim.54
  117.4 15.6 %scatter_fusion.1 = f32[8,512,256]{2,1,0:T(8,128)} fusion(f32[8,512,256]{2,1,0:T(8,128)} %broadcast_in_dim.54, s32[16]{0:T(128)S(1)} %get-tuple-element.46, f32[16,512,256]{2,1,0:T(8,128)} %copy.37), kind=kCustom, calls=%fused_computation.3 | custom fusion | flops 2097152 | bytes 25165888 | tf_op jit(solution)/shard_map/scatter-add | solution.py:44
  133.1 1.7 concatenate.12
  134.9 2.7 gather_fusion
  137.6 12.1 %convolution_bitcast_fusion.1 = f32[16,512,256]{1,2,0:T(8,128)} fusion(bf16[16,512,256]{2,1,0:T(8,128)(2,1)} %gather_fusion, bf16[16,512,512]{2,1,0:T(8,128)(2,1)} %param.8), kind=kOutput, calls=%fused_computation.17 | convolution fusion | flops 2147483648 | bytes 20971520 | tf_op jit(solution)/shard_map/tab,tbk->tak/dot_general | solution.py:37
  149.7 9.3 %copy.35 = f32[16,512,256]{2,1,0:T(8,128)} copy(f32[16,512,256]{1,2,0:T(8,128)} %convolution_bitcast_fusion.1) | data formatting | bytes 16777216 | tf_op jit(solution)/shard_map/tab,tbk->tak/dot_general | solution.py:37
  159.1 4.1 broadcast_in_dim.47
  163.1 15.9 %scatter_fusion = f32[16,512,256]{2,1,0:T(8,128)} fusion(f32[16,512,256]{2,1,0:T(8,128)} %broadcast_in_dim.47, s32[16]{0:T(128)S(1)} %fusion.37, f32[16,512,256]{2,1,0:T(8,128)} %copy.35), kind=kCustom, calls=%fused_computation.2 | custom fusion | flops 2097152 | bytes 25165888 | tf_op jit(solution)/shard_map/scatter-add | solution.py:47
  179.3 5.4 copy.43
  184.6 2.6 convert_element_type.19
  190.6 1.8 fusion.7
  193.4 136.0 %reduce-scatter.3.cloned.1.call-done = f32[2,512,256]{2,1,0:T(8,128)} async-done(((f32[16,512,256]{2,1,0:T(8,128)}), f32[2,512,256]{2,1,0:T(8,128)}) %reduce-scatter.3.cloned.1.call-update) | async-done | bytes 1048592 | tf_op jit(solution)/shard_map/reduce_scatter | solution.py:49
  331.0 2.5 convolution_bitcast_fusion.2
  333.6 130.1 %all-reduce.6.cloned.1.call-done = (f32[256,256]{0,1:T(8,128)}, f32[256,256]{0,1:T(8,128)}) async-done(((f32[256,256]{0,1:T(8,128)}, f32[256,256]{0,1:T(8,128)}), (f32[256,256]{0,1:T(8,128)}, f32[256,256]{0,1:T(8,128)})) %all-reduce.6.cloned.1.call-update) | async-done | bytes 524304 | tf_op jit(solution)/shard_map/psum | solution.py:61
  465.8 11.7 %cholesky.130 = f32[128,128]{1,0:T(8,128)S(1)} custom-call(f32[128,128]{1,0:T(8,128)S(1)} %cholesky.194), custom_call_target="Cholesky" | custom-call | tf_op jit(solution)/shard_map/jit(cholesky)/cholesky | solution.py:62
  477.6 9.8 %custom-call.13 = f32[1,128,128]{1,2,0:T(8,128)S(1)} custom-call(f32[1,128,128]{2,1,0:T(8,128)S(1)} %get-tuple-element.59), custom_call_target="InvertDiagBlocksLowerTriangular" | custom-call | tf_op jit(solution)/shard_map/jit(cholesky)/cholesky | solution.py:62
  487.9 11.7 %cholesky.147 = f32[128,128]{1,0:T(8,128)S(1)} custom-call(f32[128,128]{1,0:T(8,128)S(1)} %convolution_subtract_fusion.3), custom_call_target="Cholesky" | custom-call | tf_op jit(solution)/shard_map/jit(cholesky)/cholesky | solution.py:62
  501.7 4.0 while.4
  505.7 20.1 %custom-call.14 = f32[2,128,128]{1,2,0:T(8,128)S(1)} custom-call(f32[2,128,128]{2,1,0:T(8,128)S(1)} %get-tuple-element.18), custom_call_target="InvertDiagBlocksLowerTriangular" | custom-call | tf_op jit(solution)/shard_map/triangular_solve/custom-call.0 | solution.py:63
  528.0 1.7 fusion.10
  530.7 75.4 %all-gather.9.cloned.1.call-done = f32[8192,256]{1,0:T(8,128)} async-done(((f32[256,256]{1,0:T(8,128)}), f32[8192,256]{1,0:T(8,128)}) %all-gather.9.cloned.1.call-update) | async-done | bytes 8388624 | tf_op jit(solution)/shard_map/all_gather | solution.py:67
  606.0 3.9 reduce_sum.19
  610.2 11.7 %cholesky.164 = f32[128,128]{1,0:T(8,128)S(1)} custom-call(f32[128,128]{1,0:T(8,128)S(1)} %cholesky.197), custom_call_target="Cholesky" | custom-call | tf_op jit(solution)/shard_map/jit(cholesky)/cholesky | solution.py:68
  621.9 9.8 %custom-call.15 = f32[1,128,128]{1,2,0:T(8,128)S(1)} custom-call(f32[1,128,128]{2,1,0:T(8,128)S(1)} %get-tuple-element.55), custom_call_target="InvertDiagBlocksLowerTriangular" | custom-call | tf_op jit(solution)/shard_map/jit(cholesky)/cholesky | solution.py:68
  632.2 11.9 %cholesky.181 = f32[128,128]{1,0:T(8,128)S(1)} custom-call(f32[128,128]{1,0:T(8,128)S(1)} %convolution_subtract_fusion.2), custom_call_target="Cholesky" | custom-call | tf_op jit(solution)/shard_map/jit(cholesky)/cholesky | solution.py:68
  646.9 4.1 while.5
  651.0 19.7 %custom-call.16 = f32[2,128,128]{1,2,0:T(8,128)S(1)} custom-call(f32[2,128,128]{2,1,0:T(8,128)S(1)} %get-tuple-element.19), custom_call_target="InvertDiagBlocksLowerTriangular" | custom-call | tf_op jit(solution)/shard_map/triangular_solve/custom-call.0 | solution.py:69
  (80 shorter events, 30.3 us)
Async XLA Ops:
  7.2 78.5 %all-gather.7.cloned.1.call-start = ((), (), s32[]{:S(2)}) async-start(), calls=%async_computation.4 | async-start | bytes 4718592 | tf_op jit(solution)/shard_map/all_gather | solution.py:31
  7.9 125.2 %all-gather.5.cloned.1.call-start = ((), (), s32[]{:S(2)}) async-start(), calls=%async_computation.2 | async-start | bytes 2621440 | tf_op jit(solution)/shard_map/all_gather | solution.py:30
  8.6 184.7 %reduce-scatter.5.cloned.1.call-start = ((), (), s32[]{:S(2)}) async-start(), calls=%async_computation.5 | async-start | bytes 5242880 | tf_op jit(solution)/shard_map/reduce_scatter | solution.py:58
  133.0 196.3 %reduce-scatter.3.cloned.1.call-start = ((), (), s32[]{:S(2)}) async-start(), calls=%async_computation.3 | async-start | bytes 9437184 | tf_op jit(solution)/shard_map/reduce_scatter | solution.py:49
  179.0 284.6 %all-reduce.6.cloned.1.call-start = ((), (), s32[]{:S(2)}) async-start(), calls=%async_computation.7 | async-start | bytes 1048576 | tf_op jit(solution)/shard_map/psum | solution.py:61
  184.6 3.4 copy-start
  188.8 1.8 copy-start.1
  333.5 272.5 %all-gather.9.cloned.1.call-start = ((), (), s32[]{:S(2)}) async-start(), calls=%async_computation.6 | async-start | bytes 8650752 | tf_op jit(solution)/shard_map/all_gather | solution.py:67
  465.8 64.0 %copy-start.2 = (f32[256,256]{0,1:T(8,128)S(1)}, f32[256,256]{0,1:T(8,128)}, u32[]{:S(2)}) copy-start(f32[256,256]{0,1:T(8,128)} %get-tuple-element.43) | copy-start | bytes 786436
Sparse Core Ops, SparseCore 0:
  10.1 75.5 all-gather.6
  87.2 21.0 all-gather.4
  133.1 45.1 reduce-scatter.4
  181.8 147.4 reduce-scatter.2
  335.2 128.4 all-reduce.5
  529.9 76.0 all-gather.8
